TPU v7x, 128 devices: a whole 4x4x4 slice. The times are simulated.
128 devices in a mesh: gr: 16 (over x, y), gc: 8 (over z, core).
Axes of the slice: x: 4, y: 4, z: 4, core: 2. Of those that a mesh axis runs over, the one named last changes fastest.
Arguments:
- child_rows: float32 [8192, 12288], P('gr', 'gc'), may hold values from -1.5 to 1.5
- row_map: int32 [8192], P('gr'), may hold values from 0 to 8191, as said below
- stair: int32 [64], replicated, may hold values from 0 to 896, as said below
Outputs:
- factor: float32 [1024, 12288], P('gr', 'gc')
- projected: float32 [8192, 12288], P('gr', 'gc')
Inputs may be any that keep to these rules, and one draw needn't show every extreme that they name: row_map is a permutation of 0 to 8191. Of the 512 rows of one index of gr, at most 152 go to the rows of any one index of gr (row_map // 512), and some index of gr sends exactly 152 to one index. stair is nondecreasing and a multiple of 128; the first quarter of the blocks is 0 and the last block holds 896.
All inputs are finite; a program needn't handle non-finite values.
Results may differ from a plain program's by a relative error of at most 0.0003.
Values sent between devices are 32-bit elements; how exact they have to be, the bound alone decides.
A program may use at most 128 MiB of HBM per device.

v0:
```python
import jax
import jax.numpy as jnp
from jax import lax
from jax.sharding import PartitionSpec as P

PANEL = 512
NPANEL = 2
STAIR_BLOCK = 128


def spread(value, axis, source):
    kept = jnp.where(lax.axis_index(axis) == source, value, 0).astype(value.dtype)
    return lax.psum(kept, axis)


def pack_rows(values, targets, groups):
    rows_dev = values.shape[0]
    base_rows = 3 * rows_dev // (4 * groups)
    capacity = rows_dev - base_rows * (groups - 1)
    target_dev = targets // rows_dev
    target_row = targets % rows_dev
    onehot = (target_dev[:, None] == jnp.arange(groups, dtype=jnp.int32)[None, :]).astype(jnp.int32)
    rank_within = jnp.sum((jnp.cumsum(onehot, axis=0) - onehot) * onehot, axis=1)
    buffer_index = target_dev * capacity + rank_within
    source_row = (
        jnp.full((groups * capacity,), rows_dev, jnp.int32)
        .at[buffer_index]
        .set(jnp.arange(rows_dev, dtype=jnp.int32))
    )
    sent_rows = jnp.take(values, source_row, axis=0, mode="fill", fill_value=0.0)
    sent_slots = (
        jnp.full((groups * capacity,), rows_dev, jnp.int32).at[buffer_index].set(target_row)
    )
    return (
        sent_rows.reshape(groups, capacity, values.shape[1]),
        sent_slots.reshape(groups, capacity),
    )


def place_rows(recv_rows, recv_slots, rows_dev):
    flat_rows = recv_rows.reshape(-1, recv_rows.shape[-1])
    flat_slots = recv_slots.reshape(-1)
    where_from = (
        jnp.zeros((rows_dev,), jnp.int32)
        .at[flat_slots]
        .set(jnp.arange(flat_slots.shape[0], dtype=jnp.int32), mode="drop")
    )
    return jnp.take(flat_rows, where_from, axis=0)


def matmul(left, right):
    return jnp.dot(left, right, precision=lax.Precision.HIGHEST, preferred_element_type=jnp.float32)


def high(left, right, contract):
    return lax.dot_general(
        left,
        right,
        (contract, ((), ())),
        precision=lax.Precision.HIGH,
        preferred_element_type=jnp.float32,
    )


def inverse_factor(upper, size):
    count = upper.shape[0] // size
    eye = jnp.eye(size, dtype=upper.dtype)
    done = jnp.zeros((upper.shape[0], 0), upper.dtype)
    rest = upper
    rows = []
    for k in range(count):
        lower = lax.linalg.cholesky(rest[:size, :size], symmetrize_input=False)
        small = lax.linalg.triangular_solve(lower, eye, left_side=True, lower=True)
        scaled = matmul(small, jnp.concatenate([rest[:size, size:], done[:size]], axis=1))
        right = rest.shape[1] - size
        rows.append(
            jnp.concatenate(
                [scaled[:, right:], small, jnp.zeros((size, right), upper.dtype)], axis=1
            )
        )
        if right > 0:
            terms = jnp.concatenate([scaled, small], axis=1)
            taken = lax.dot_general(
                scaled[:, :right],
                terms,
                (((0,), (0,)), ((), ())),
                precision=lax.Precision.HIGHEST,
                preferred_element_type=jnp.float32,
            )
            rest = rest[size:, size:] - taken[:, :right]
            fresh = jnp.zeros((right, size), upper.dtype)
            done = jnp.concatenate([done[size:], fresh], axis=1) - taken[:, right:]
    return jnp.concatenate(rows, axis=0)


def shards(child_rows, row_map, stair):
    groups = lax.axis_size("gr")
    rows_dev, cols_dev = child_rows.shape
    wide = NPANEL * PANEL
    half = PANEL // 2
    columns = lax.axis_index("gc") * cols_dev + jnp.arange(cols_dev, dtype=jnp.int32)
    limits = jnp.take(stair, row_map // STAIR_BLOCK)
    masked = jnp.where(columns[None, :] >= limits[:, None], child_rows, jnp.zeros_like(child_rows))
    sent_rows, sent_slots = pack_rows(masked, row_map, groups)
    recv_slots = lax.all_to_all(sent_slots, "gr", split_axis=0, concat_axis=0, tiled=True)
    panel = spread(masked[:, :wide], "gc", 0)
    first, second = (panel[:, :PANEL], panel[:, PANEL:])
    local = high(panel, masked, ((0,), (0,)))
    top = matmul(first.T, panel)
    low = matmul(second.T, second)
    left = jnp.concatenate([top[:, :PANEL], top[:, PANEL:]], axis=0)
    low = jnp.concatenate([low[:, :half], low[:, half:]], axis=0)
    sums = lax.psum(jnp.concatenate([local, left, low], axis=1), "gr")
    sums, sent_rows = lax.optimization_barrier((sums, sent_rows))
    recv_rows = lax.all_to_all(sent_rows, "gr", split_axis=0, concat_axis=0, tiled=True)
    products = sums[:, :cols_dev]
    gram = sums[:, cols_dev:]
    low = jnp.concatenate([gram[:PANEL, PANEL:], gram[PANEL:, PANEL:]], axis=1)
    top = jnp.concatenate([gram[:PANEL, :PANEL], gram[PANEL:, :PANEL]], axis=1)
    low = jnp.concatenate([jnp.zeros_like(low), low], axis=1)
    inverse = inverse_factor(jnp.concatenate([top, low], axis=0), STAIR_BLOCK)
    front = place_rows(recv_rows, recv_slots, rows_dev)
    front_panel = spread(front[:, :wide], "gc", 0)
    basis = high(front_panel, inverse, ((1,), (1,)))
    stacked = high(inverse, products, ((1,), (0,)))
    projected = front - high(basis, stacked, ((1,), (0,)))
    share_rows = wide // groups
    factor = lax.dynamic_slice_in_dim(stacked, lax.axis_index("gr") * share_rows, share_rows, 0)
    return (factor, projected)


def solution(mesh):
    placed = (P("gr", "gc"), P("gr"), P())
    return jax.shard_map(
        shards,
        mesh=mesh,
        in_specs=placed,
        out_specs=(P("gr", "gc"), P("gr", "gc")),
        check_vma=False,
    )
```

profile of v0, /device:TPU:0, one launch (start us, length us, event | category | flops | bytes accessed | tf_op | source)
XLA Modules:
  0.0 674.6 jit_solution(3320407137401549536)
XLA Ops:
  15.0 40.6 %select_select_fusion.8 = s32[512]{0:T(512)S(1)} fusion(s32[512]{0:T(512)} %param.7, s32[]{:T(128)} %bitcast, s32[]{:T(128)} %bitcast.1, s32[]{:T(128)} %bitcast.2, s32[]{:T(128)} %bitcast.3, s32[]{:T(128)} %bitcast.4, s32[]{:T(128)} %bitcast.5, s32[]{:T(128)} %bitcast.6, s32[]{:T(128)} %bitcast.7, s32[]{:T(128)} %bitcast.8, s32[]{:T(128)} %bitcast.9, ...), kind=kLoop, calls=%fused_computation.189 | loop fusion | flops 75776 | bytes 4352 | tf_op jit(solution)/shard_map/jit(_take)/select_n | solution.py:102
  59.5 68.5 %all-reduce.11.cloned.1.call-done = f32[512,1024]{1,0:T(8,128)} async-done(((f32[512,1024]{1,0:T(8,128)}), f32[512,1024]{1,0:T(8,128)}) %all-reduce.11.cloned.1.call-update) | async-done | bytes 2097168 | tf_op jit(solution)/shard_map/psum | solution.py:13
  163.1 10.0 %gather_fusion = f32[2432,1536]{1,0:T(8,128)} fusion(f32[512,1536]{1,0:T(8,128)S(1)} %compare_select_fusion, s32[3072]{0:T(1024)S(1)} %pad_clamp_fusion), kind=kCustom, calls=%fused_computation | custom fusion | bytes 29894144 | tf_op jit(solution)/shard_map/jit(_take)/gather | solution.py:30
  173.1 12.4 %broadcast_select_fusion = f32[16,152,1536]{2,1,0:T(8,128)} fusion(f32[16,152,1536]{2,1,0:T(8,128)} %bitcast.146, pred[16,152]{1,0:T(8,128)(4,1)S(1)} %broadcast_in_dim.83), kind=kLoop, calls=%fused_computation.6 | loop fusion | flops 3735552 | bytes 29886848 | tf_op jit(solution)/shard_map/jit(_take)/select_n | solution.py:30
  186.4 12.3 %scatter_custom_fusion.2 = s32[512]{0:T(512)S(1)} fusion(s32[2432]{0:T(1024)S(1)} %fusion.105, s32[2432]{0:T(1024)S(1)} %iota.147, s32[]{:T(128)} %constant.119.clone.1), kind=kCustom, calls=%fused_computation.200 | custom fusion | bytes 2052 | tf_op jit(solution)/shard_map/scatter | solution.py:46
  199.8 98.3 %all-reduce.13.cloned.1.call-done = f32[1024,2304]{1,0:T(8,128)} async-done(((f32[1024,2304]{1,0:T(8,128)}), f32[1024,2304]{1,0:T(8,128)}) %all-reduce.13.cloned.1.call-update) | async-done | bytes 9437200 | tf_op jit(solution)/shard_map/psum | solution.py:113
  306.3 11.7 %custom-call.20 = f32[128,128]{1,0:T(8,128)S(1)} custom-call(f32[128,128]{1,0:T(8,128)S(1)} %slice.241), custom_call_target="Cholesky" | custom-call | tf_op jit(solution)/shard_map/cholesky/custom-call.1 | solution.py:72
  319.4 9.8 %custom-call.21 = f32[1,128,128]{1,2,0:T(8,128)S(1)} custom-call(f32[1,128,128]{2,1,0:T(8,128)S(1)} %fusion.84), custom_call_target="InvertDiagBlocksLowerTriangular" | custom-call | tf_op jit(solution)/shard_map/triangular_solve/custom-call.0 | solution.py:73
  336.6 11.9 %custom-call.22 = f32[128,128]{1,0:T(8,128)S(1)} custom-call(f32[128,128]{1,0:T(8,128)S(1)} %slice.384), custom_call_target="Cholesky" | custom-call | tf_op jit(solution)/shard_map/cholesky/custom-call.1 | solution.py:72
  349.8 9.8 %custom-call.23 = f32[1,128,128]{1,2,0:T(8,128)S(1)} custom-call(f32[1,128,128]{2,1,0:T(8,128)S(1)} %fusion.85), custom_call_target="InvertDiagBlocksLowerTriangular" | custom-call | tf_op jit(solution)/shard_map/triangular_solve/custom-call.0 | solution.py:73
  367.2 11.9 %custom-call.24 = f32[128,128]{1,0:T(8,128)S(1)} custom-call(f32[128,128]{1,0:T(8,128)S(1)} %slice.392), custom_call_target="Cholesky" | custom-call | tf_op jit(solution)/shard_map/cholesky/custom-call.1 | solution.py:72
  380.5 9.8 %custom-call.25 = f32[1,128,128]{1,2,0:T(8,128)S(1)} custom-call(f32[1,128,128]{2,1,0:T(8,128)S(1)} %fusion.86), custom_call_target="InvertDiagBlocksLowerTriangular" | custom-call | tf_op jit(solution)/shard_map/triangular_solve/custom-call.0 | solution.py:73
  395.3 11.7 %custom-call.26 = f32[128,128]{1,0:T(8,128)S(1)} custom-call(f32[128,128]{1,0:T(8,128)S(1)} %slice.401), custom_call_target="Cholesky" | custom-call | tf_op jit(solution)/shard_map/cholesky/custom-call.1 | solution.py:72
  408.4 9.8 %custom-call.27 = f32[1,128,128]{1,2,0:T(8,128)S(1)} custom-call(f32[1,128,128]{2,1,0:T(8,128)S(1)} %fusion.87), custom_call_target="InvertDiagBlocksLowerTriangular" | custom-call | tf_op jit(solution)/shard_map/triangular_solve/custom-call.0 | solution.py:73
  422.6 11.7 %custom-call.28 = f32[128,128]{1,0:T(8,128)S(1)} custom-call(f32[128,128]{1,0:T(8,128)S(1)} %slice.410), custom_call_target="Cholesky" | custom-call | tf_op jit(solution)/shard_map/cholesky/custom-call.1 | solution.py:72
  435.6 9.8 %custom-call.29 = f32[1,128,128]{1,2,0:T(8,128)S(1)} custom-call(f32[1,128,128]{2,1,0:T(8,128)S(1)} %fusion.88), custom_call_target="InvertDiagBlocksLowerTriangular" | custom-call | tf_op jit(solution)/shard_map/triangular_solve/custom-call.0 | solution.py:73
  448.2 11.9 %custom-call.30 = f32[128,128]{1,0:T(8,128)S(1)} custom-call(f32[128,128]{1,0:T(8,128)S(1)} %slice.419), custom_call_target="Cholesky" | custom-call | tf_op jit(solution)/shard_map/cholesky/custom-call.1 | solution.py:72
  474.0 11.7 %custom-call.32 = f32[128,128]{1,0:T(8,128)S(1)} custom-call(f32[128,128]{1,0:T(8,128)S(1)} %get-tuple-element.21), custom_call_target="Cholesky" | custom-call | tf_op jit(solution)/shard_map/cholesky/custom-call.1 | solution.py:72
  487.0 10.0 %custom-call.33 = f32[1,128,128]{1,2,0:T(8,128)S(1)} custom-call(f32[1,128,128]{2,1,0:T(8,128)S(1)} %fusion.90), custom_call_target="InvertDiagBlocksLowerTriangular" | custom-call | tf_op jit(solution)/shard_map/triangular_solve/custom-call.0 | solution.py:73
  500.9 11.7 %custom-call.34 = f32[128,128]{1,0:T(8,128)S(1)} custom-call(f32[128,128]{1,0:T(8,128)S(1)} %slice_subtract_fusion.14), custom_call_target="Cholesky" | custom-call | tf_op jit(solution)/shard_map/cholesky/custom-call.1 | solution.py:72
  533.5 31.4 %all-to-all-done.1 = f32[16,152,1536]{2,1,0:T(8,128)} async-done(((f32[16,152,1536]{2,1,0:T(8,128)}), f32[16,152,1536]{2,1,0:T(8,128)}, u32[]{:S(2)}, u32[]{:S(2)}) %all-to-all-start.1) | async-done | bytes 14942240 | tf_op jit(solution)/shard_map/all_to_all | solution.py:115
  564.9 10.0 %gather_fusion.1 = f32[512,1536]{1,0:T(8,128)} fusion(f32[2432,1536]{1,0:T(8,128)} %bitcast.83, s32[1024]{0:T(1024)S(1)} %copy-done.27), kind=kCustom, calls=%fused_computation.1 | custom fusion | bytes 6293504 | tf_op jit(solution)/shard_map/jit(_take)/gather | solution.py:48
  578.7 13.7 %fusion = f32[1024,1536]{1,0:T(8,128)S(1)} fusion(f32[1024,1024]{1,0:T(8,128)} %maximum_dynamic-update-slice_fusion, f32[1024,2304]{1,0:T(8,128)} %all-reduce.13.cloned.1.call-done), kind=kOutput, calls=%fused_computation.7 | convolution fusion | flops 9663676416 | bytes 16777216 | tf_op jit(solution)/shard_map/dot_general | solution.py:56
  595.8 57.7 %all-reduce.15.cloned.1.call-done = f32[512,1024]{1,0:T(8,128)} async-done(((f32[512,1024]{1,0:T(8,128)}), f32[512,1024]{1,0:T(8,128)}) %all-reduce.15.cloned.1.call-update) | async-done | bytes 2097168 | tf_op jit(solution)/shard_map/psum | solution.py:13
  (233 shorter events, 150.9 us)
Async XLA Ops:
  7.2 120.8 %all-reduce.11.cloned.1.call-start = ((), (), s32[]{:S(2)}) async-start(), calls=%async_computation.2 | async-start | bytes 4194304 | tf_op jit(solution)/shard_map/psum | solution.py:13
  59.4 238.8 %all-reduce.13.cloned.1.call-start = ((), (), s32[]{:S(2)}) async-start(), calls=%async_computation.3 | async-start | bytes 18874368 | tf_op jit(solution)/shard_map/psum | solution.py:113
  153.6 32.5 %all-to-all-start = ((s32[16,1,152]{2,1,0:T(1,128)}), s32[16,1,152]{2,1,0:T(1,128)S(1)}, u32[]{:S(2)}, u32[]{:S(2)}) async-start(s32[16,1,152]{2,1,0:T(1,128)} %all_to_all.9), calls=%async_computation | async-start | bytes 32768 | tf_op jit(solution)/shard_map/all_to_all | solution.py:105
  300.7 28.8 %copy-start.1 = (f32[512,512]{1,0:T(8,128)}, f32[512,512]{1,0:T(8,128)S(1)}, u32[]{:S(2)}) copy-start(f32[512,512]{1,0:T(8,128)S(1)} %get-tuple-element.10) | copy-start | bytes 3145732
  300.7 28.8 %copy-start.3 = (f32[512,512]{1,0:T(8,128)}, f32[512,512]{1,0:T(8,128)S(1)}, u32[]{:S(2)}) copy-start(f32[512,512]{1,0:T(8,128)S(1)} %get-tuple-element.11) | copy-start | bytes 3145732
  300.8 264.2 %all-to-all-start.1 = ((f32[16,152,1536]{2,1,0:T(8,128)}), f32[16,152,1536]{2,1,0:T(8,128)}, u32[]{:S(2)}, u32[]{:S(2)}) async-start(f32[16,152,1536]{2,1,0:T(8,128)} %broadcast_select_fusion), calls=%async_computation.1 | async-start | bytes 29884416 | tf_op jit(solution)/shard_map/all_to_all | solution.py:115
  305.9 347.7 %all-reduce.15.cloned.1.call-start = ((), (), s32[]{:S(2)}) async-start(), calls=%async_computation.4 | async-start | bytes 4194304 | tf_op jit(solution)/shard_map/psum | solution.py:13
  360.0 4.5 copy-start.15
  360.0 4.3 copy-start.14
  365.8 28.4 %copy-start.10 = (f32[640,256]{1,0:T(8,128)S(1)}, f32[640,256]{1,0:T(8,128)}, u32[]{:S(2)}) copy-start(f32[640,256]{1,0:T(8,128)} %slice.403) | copy-start | bytes 1966084
  395.3 26.8 %slice-start = ((f32[640,384]{1,0:T(8,128)}), f32[512,384]{1,0:T(8,128)S(1)}, s32[]{:S(2)}) async-start(f32[640,384]{1,0:T(8,128)} %copy-done.9), calls=%async_computation.5 | async-start | bytes 1572864 | tf_op jit(solution)/shard_map/slice | solution.py:92
  471.7 25.6 %copy-start.17 = (f32[128,128]{1,0:T(8,128)}, f32[128,128]{1,0:T(8,128)S(1)}, u32[]{:S(2)}) copy-start(f32[128,128]{1,0:T(8,128)S(1)} %copy.27) | copy-start | bytes 196612
  472.3 25.8 %copy-start.13 = (f32[128,896]{1,0:T(8,128)}, f32[128,896]{1,0:T(8,128)S(1)}, u32[]{:S(2)}) copy-start(f32[128,896]{1,0:T(8,128)S(1)} %fusion.54) | copy-start | bytes 1376260
  497.9 27.1 %slice-start.1 = ((f32[128,896]{1,0:T(8,128)}), f32[128,128]{1,0:T(8,128)S(1)}, s32[]{:S(2)}) async-start(f32[128,896]{1,0:T(8,128)} %copy-done.11), calls=%async_computation.6 | async-start | bytes 131072 | tf_op jit(solution)/shard_map/slice | solution.py:78
  497.9 27.1 %copy-start.16 = (f32[128,128]{1,0:T(8,128)S(1)}, f32[128,128]{1,0:T(8,128)}, u32[]{:S(2)}) copy-start(f32[128,128]{1,0:T(8,128)} %copy-done.15) | copy-start | bytes 196612
  498.0 27.9 %copy-start.22 = (f32[128,128]{1,0:T(8,128)S(1)}, f32[128,128]{1,0:T(8,128)}, u32[]{:S(2)}) copy-start(f32[128,128]{1,0:T(8,128)} %copy-done.21) | copy-start | bytes 196612
  498.0 29.7 %copy-start.20 = (f32[128,128]{1,0:T(8,128)S(1)}, f32[128,128]{1,0:T(8,128)}, u32[]{:S(2)}) copy-start(f32[128,128]{1,0:T(8,128)} %copy-done.19) | copy-start | bytes 196612
  498.1 31.4 %slice-start.2 = ((f32[128,896]{1,0:T(8,128)}), f32[128,512]{1,0:T(8,128)S(1)}, s32[]{:S(2)}) async-start(f32[128,896]{1,0:T(8,128)} %copy-done.12), calls=%async_computation.7 | async-start | bytes 524288 | tf_op jit(solution)/shard_map/slice | solution.py:78
  498.1 31.4 %copy-start.24 = (f32[128,128]{1,0:T(8,128)S(1)}, f32[128,128]{1,0:T(8,128)}, u32[]{:S(2)}) copy-start(f32[128,128]{1,0:T(8,128)} %copy-done.23) | copy-start | bytes 196612
  498.7 31.6 %slice-start.3 = ((f32[128,896]{1,0:T(8,128)}), f32[128,640]{1,0:T(8,128)S(1)}, s32[]{:S(2)}) async-start(f32[128,896]{1,0:T(8,128)} %copy-done.13), calls=%async_computation.8 | async-start | bytes 655360 | tf_op jit(solution)/shard_map/slice | solution.py:78
  498.7 31.6 %copy-start.18 = (f32[128,128]{1,0:T(8,128)S(1)}, f32[128,128]{1,0:T(8,128)}, u32[]{:S(2)}) copy-start(f32[128,128]{1,0:T(8,128)} %copy-done.17) | copy-start | bytes 196612
  527.7 37.2 %copy-start.27 = (s32[1024]{0:T(1024)S(1)}, s32[1024]{0:T(1024)}, u32[]{:S(2)}) copy-start(s32[1024]{0:T(1024)} %pad_clamp_fusion.1) | copy-start | bytes 12292
  564.9 10.0 %copy-start.29 = (pred[512]{0:T(512)(128)(4,1)S(1)}, pred[512]{0:T(512)(128)(4,1)}, u32[]{:S(2)}) copy-start(pred[512]{0:T(512)(128)(4,1)} %compare_and_fusion.1) | copy-start | bytes 1540
  653.5 6.8 %copy-start.8 = (f32[1024,1536]{1,0:T(8,128)S(1)}, f32[1024,1536]{1,0:T(8,128)}, u32[]{:S(2)}) copy-start(f32[1024,1536]{1,0:T(8,128)} %copy-done.7) | copy-start | bytes 18874372
  (15 other events, 28.4 us)
Sparse Core Ops, SparseCore 0:
  59.5 68.3 all-reduce.10
  148.4 149.7 all-reduce.12
  578.8 74.6 all-reduce.14
where the time goes:
time: 685 us; the launch traced here: 675 us
  other arithmetic  264 us (39%)
  waiting for transfers between devices  256 us (37%)
  local copies, waits for them, and re-layouts  64.7 us (9%)
  matrix products  62.4 us (9%)
  between operations  15.4 us (2%)
  starting transfers between devices  12.4 us (2%)
    psum x2, waiting for transfers between devices, spread(): return lax.psum(kept, axis)  126 us
    another operation x24, other arithmetic, inverse_factor(): lower = lax.linalg.cholesky(rest[:size, :size], symmetrize_input=False)  99.8 us
    psum x1, waiting for transfers between devices, shards(): sums = lax.psum(jnp.concatenate([local, left, low], axis=1), 'gr')  98.3 us
    another operation x16, other arithmetic, inverse_factor(): small = lax.linalg.triangular_solve(lower, eye, left_side=True, lower=True)  83.9 us
    select_n x1, other arithmetic, shards(): limits = jnp.take(stair, row_map // STAIR_BLOCK)  40.6 us
    dot_general x4, matrix products, high(): lax.dot_general(left, right, (contract, ((), ())), precision=lax.Precisio...  33.4 us
    all_to_all x1, waiting for transfers between devices, shards(): lax.all_to_all(sent_rows, 'gr', split_axis=0, concat_axis=0, tiled=True)  31.4 us
    dot_general x10, matrix products, matmul(): jnp.dot(left, right, precision=lax.Precision.HIGHEST, preferred_element_t...  14 us
  transfers between devices with their start and end apart: 5, of which 4 were waited for; matrix products, arithmetic and copies ran while one was open for 42% of the time, Pallas kernels for 0%

commit v1 on v0

--- a/solution.py
+++ b/solution.py
@@ -10,7 +10,7 @@
 
 def spread(value, axis, source):
     kept = jnp.where(lax.axis_index(axis) == source, value, 0).astype(value.dtype)
-    return lax.psum(kept, axis)
+    return jnp.sum(lax.all_gather(kept, axis), axis=0)
 
 
 def pack_rows(values, targets, groups):

time: 685 us -> 956 us (1.40)
  the two profiles are of different devices: /device:TPU:0 before, /device:TPU:20 now
where the time goes in v1:
time: 956 us; the launch traced here: 943 us
  waiting for transfers between devices  452 us (47%)
  other arithmetic  305 us (32%)
  local copies, waits for them, and re-layouts  81.6 us (9%)
  matrix products  75 us (8%)
  between operations  15.4 us (2%)
  starting transfers between devices  15 us (2%)
    all_to_all x1, waiting for transfers between devices, shards(): lax.all_to_all(sent_rows, 'gr', split_axis=0, concat_axis=0, tiled=True)  254 us
    psum x1, waiting for transfers between devices, shards(): sums = lax.psum(jnp.concatenate([local, left, low], axis=1), 'gr')  111 us
    another operation x24, other arithmetic, inverse_factor(): lower = lax.linalg.cholesky(rest[:size, :size], symmetrize_input=False)  110 us
    another operation x16, other arithmetic, inverse_factor(): small = lax.linalg.triangular_solve(lower, eye, left_side=True, lower=True)  97.8 us
    all_gather x2, waiting for transfers between devices, spread(): return jnp.sum(lax.all_gather(kept, axis), axis=0)  87.4 us
    select_n x1, other arithmetic, shards(): limits = jnp.take(stair, row_map // STAIR_BLOCK)  40.6 us
    dot_general x4, matrix products, high(): lax.dot_general(left, right, (contract, ((), ())), precision=lax.Precisio...  33.7 us
  transfers between devices with their start and end apart: 5, of which 3 were waited for; matrix products, arithmetic and copies ran while one was open for 35% of the time, Pallas kernels for 0%

profile of v1, /device:TPU:20, one launch (start us, length us, event | category | flops | bytes accessed | tf_op | source)
XLA Modules:
  0.0 943.4 jit_solution(2402295190747168783)
XLA Ops:
  15.0 40.6 %select_select_fusion.8 = s32[512]{0:T(512)S(1)} fusion(s32[512]{0:T(512)} %param.7, s32[]{:T(128)} %bitcast, s32[]{:T(128)} %bitcast.1, s32[]{:T(128)} %bitcast.2, s32[]{:T(128)} %bitcast.3, s32[]{:T(128)} %bitcast.4, s32[]{:T(128)} %bitcast.5, s32[]{:T(128)} %bitcast.6, s32[]{:T(128)} %bitcast.7, s32[]{:T(128)} %bitcast.8, s32[]{:T(128)} %bitcast.9, ...), kind=kLoop, calls=%fused_computation.189 | loop fusion | flops 75776 | bytes 4352 | tf_op jit(solution)/shard_map/jit(_take)/select_n | solution.py:102
  59.5 87.4 %all-gather.5.cloned.1.call-done = f32[4096,1024]{1,0:T(8,128)} async-done(((f32[512,1024]{1,0:T(8,128)}), f32[4096,1024]{1,0:T(8,128)}) %all-gather.5.cloned.1.call-update) | async-done | bytes 16777232 | tf_op jit(solution)/shard_map/all_gather | solution.py:13
  191.8 10.1 %gather_fusion = f32[2432,1536]{1,0:T(8,128)} fusion(f32[512,1536]{1,0:T(8,128)S(1)} %compare_select_fusion, s32[3072]{0:T(1024)S(1)} %pad_clamp_fusion), kind=kCustom, calls=%fused_computation | custom fusion | bytes 29894144 | tf_op jit(solution)/shard_map/jit(_take)/gather | solution.py:30
  201.9 12.7 %broadcast_select_fusion = f32[16,152,1536]{2,1,0:T(8,128)} fusion(f32[16,152,1536]{2,1,0:T(8,128)} %bitcast.148, pred[16,152]{1,0:T(8,128)(4,1)S(1)} %broadcast_in_dim.83), kind=kLoop, calls=%fused_computation.6 | loop fusion | flops 3735552 | bytes 29886848 | tf_op jit(solution)/shard_map/jit(_take)/select_n | solution.py:30
  214.6 110.6 %all-reduce.9.cloned.1.call-done = f32[1024,2304]{1,0:T(8,128)} async-done(((f32[1024,2304]{1,0:T(8,128)}), f32[1024,2304]{1,0:T(8,128)}) %all-reduce.9.cloned.1.call-update) | async-done | bytes 9437200 | tf_op jit(solution)/shard_map/psum | solution.py:113
  333.1 12.3 %scatter_custom_fusion.2 = s32[512]{0:T(512)S(1)} fusion(s32[2432]{0:T(1024)S(1)} %fusion.105, s32[2432]{0:T(1024)S(1)} %iota.147, s32[]{:T(128)} %constant.120.clone.1), kind=kCustom, calls=%fused_computation.200 | custom fusion | bytes 2052 | tf_op jit(solution)/shard_map/scatter | solution.py:46
  345.5 253.6 %all-to-all-done.1 = f32[16,152,1536]{2,1,0:T(8,128)} async-done(((f32[16,152,1536]{2,1,0:T(8,128)}), f32[16,152,1536]{2,1,0:T(8,128)}, u32[]{:S(2)}, u32[]{:S(2)}) %all-to-all-start.1) | async-done | bytes 14942240 | tf_op jit(solution)/shard_map/all_to_all | solution.py:115
  599.1 10.0 %gather_fusion.1 = f32[512,1536]{1,0:T(8,128)} fusion(f32[2432,1536]{1,0:T(8,128)} %bitcast.84, s32[1024]{0:T(1024)S(1)} %pad_clamp_fusion.1), kind=kCustom, calls=%fused_computation.1 | custom fusion | bytes 6293504 | tf_op jit(solution)/shard_map/jit(_take)/gather | solution.py:48
  614.3 11.7 %custom-call.20 = f32[128,128]{1,0:T(8,128)S(1)} custom-call(f32[128,128]{1,0:T(8,128)S(1)} %slice.241), custom_call_target="Cholesky" | custom-call | tf_op jit(solution)/shard_map/cholesky/custom-call.1 | solution.py:72
  627.4 9.8 %custom-call.21 = f32[1,128,128]{1,2,0:T(8,128)S(1)} custom-call(f32[1,128,128]{2,1,0:T(8,128)S(1)} %fusion.84), custom_call_target="InvertDiagBlocksLowerTriangular" | custom-call | tf_op jit(solution)/shard_map/triangular_solve/custom-call.0 | solution.py:73
  647.4 12.1 %custom-call.22 = f32[128,128]{1,0:T(8,128)S(1)} custom-call(f32[128,128]{1,0:T(8,128)S(1)} %slice.384), custom_call_target="Cholesky" | custom-call | tf_op jit(solution)/shard_map/cholesky/custom-call.1 | solution.py:72
  679.1 13.3 %custom-call.24 = f32[128,128]{1,0:T(8,128)} custom-call(f32[128,128]{1,0:T(8,128)} %slice.392), custom_call_target="Cholesky" | custom-call | tf_op jit(solution)/shard_map/cholesky/custom-call.1 | solution.py:72
  696.0 11.3 %custom-call.25 = f32[1,128,128]{1,2,0:T(8,128)} custom-call(f32[1,128,128]{2,1,0:T(8,128)} %fusion.86), custom_call_target="InvertDiagBlocksLowerTriangular" | custom-call | tf_op jit(solution)/shard_map/triangular_solve/custom-call.0 | solution.py:73
  719.2 12.5 %custom-call.26 = f32[128,128]{1,0:T(8,128)S(1)} custom-call(f32[128,128]{1,0:T(8,128)} %slice.401), custom_call_target="Cholesky" | custom-call | tf_op jit(solution)/shard_map/cholesky/custom-call.1 | solution.py:72
  733.8 10.8 %custom-call.27 = f32[1,128,128]{1,2,0:T(8,128)S(1)} custom-call(f32[1,128,128]{2,1,0:T(8,128)} %fusion.87), custom_call_target="InvertDiagBlocksLowerTriangular" | custom-call | tf_op jit(solution)/shard_map/triangular_solve/custom-call.0 | solution.py:73
  753.7 12.5 %custom-call.28 = f32[128,128]{1,0:T(8,128)S(1)} custom-call(f32[128,128]{1,0:T(8,128)} %slice.410), custom_call_target="Cholesky" | custom-call | tf_op jit(solution)/shard_map/cholesky/custom-call.1 | solution.py:72
  768.1 10.6 %custom-call.29 = f32[1,128,128]{1,2,0:T(8,128)S(1)} custom-call(f32[1,128,128]{2,1,0:T(8,128)} %fusion.88), custom_call_target="InvertDiagBlocksLowerTriangular" | custom-call | tf_op jit(solution)/shard_map/triangular_solve/custom-call.0 | solution.py:73
  786.3 13.6 %custom-call.30 = f32[128,128]{1,0:T(8,128)} custom-call(f32[128,128]{1,0:T(8,128)} %slice.419), custom_call_target="Cholesky" | custom-call | tf_op jit(solution)/shard_map/cholesky/custom-call.1 | solution.py:72
  803.5 11.3 %custom-call.31 = f32[1,128,128]{1,2,0:T(8,128)} custom-call(f32[1,128,128]{2,1,0:T(8,128)} %fusion.89), custom_call_target="InvertDiagBlocksLowerTriangular" | custom-call | tf_op jit(solution)/shard_map/triangular_solve/custom-call.0 | solution.py:73
  824.3 12.5 %custom-call.32 = f32[128,128]{1,0:T(8,128)S(1)} custom-call(f32[128,128]{1,0:T(8,128)} %get-tuple-element.21), custom_call_target="Cholesky" | custom-call | tf_op jit(solution)/shard_map/cholesky/custom-call.1 | solution.py:72
  838.9 11.4 %custom-call.33 = f32[1,128,128]{1,2,0:T(8,128)} custom-call(f32[1,128,128]{2,1,0:T(8,128)} %fusion.90), custom_call_target="InvertDiagBlocksLowerTriangular" | custom-call | tf_op jit(solution)/shard_map/triangular_solve/custom-call.0 | solution.py:73
  859.5 13.2 %custom-call.34 = f32[128,128]{1,0:T(8,128)} custom-call(f32[128,128]{1,0:T(8,128)} %slice_subtract_fusion.14), custom_call_target="Cholesky" | custom-call | tf_op jit(solution)/shard_map/cholesky/custom-call.1 | solution.py:72
  876.5 11.3 %custom-call.35 = f32[1,128,128]{1,2,0:T(8,128)} custom-call(f32[1,128,128]{2,1,0:T(8,128)} %fusion.91), custom_call_target="InvertDiagBlocksLowerTriangular" | custom-call | tf_op jit(solution)/shard_map/triangular_solve/custom-call.0 | solution.py:73
  895.8 13.9 %fusion = f32[1024,1536]{1,0:T(8,128)S(1)} fusion(f32[1024,1024]{1,0:T(8,128)S(1)} %maximum_dynamic-update-slice_fusion, f32[1024,2304]{1,0:T(8,128)} %all-reduce.9.cloned.1.call-done), kind=kOutput, calls=%fused_computation.7 | convolution fusion | flops 9663676416 | bytes 16777216 | tf_op jit(solution)/shard_map/dot_general | solution.py:56
  (251 shorter events, 198.8 us)
Async XLA Ops:
  7.2 139.7 %all-gather.5.cloned.1.call-start = ((), (), s32[]{:S(2)}) async-start(), calls=%async_computation.3 | async-start | bytes 18874368 | tf_op jit(solution)/shard_map/all_gather | solution.py:13
  59.4 265.7 %all-reduce.9.cloned.1.call-start = ((), (), s32[]{:S(2)}) async-start(), calls=%async_computation.2 | async-start | bytes 18874368 | tf_op jit(solution)/shard_map/psum | solution.py:113
  181.9 143.2 %all-to-all-start = ((s32[16,1,152]{2,1,0:T(1,128)}), s32[16,1,152]{2,1,0:T(1,128)S(1)}, u32[]{:S(2)}, u32[]{:S(2)}) async-start(s32[16,1,152]{2,1,0:T(1,128)} %all_to_all.9), calls=%async_computation | async-start | bytes 32768 | tf_op jit(solution)/shard_map/all_to_all | solution.py:105
  325.2 273.9 %all-to-all-start.1 = ((f32[16,152,1536]{2,1,0:T(8,128)}), f32[16,152,1536]{2,1,0:T(8,128)}, u32[]{:S(2)}, u32[]{:S(2)}) async-start(f32[16,152,1536]{2,1,0:T(8,128)} %broadcast_select_fusion), calls=%async_computation.1 | async-start | bytes 29884416 | tf_op jit(solution)/shard_map/all_to_all | solution.py:115
  332.9 580.3 %all-gather.7.cloned.1.call-start = ((), (), s32[]{:S(2)}) async-start(), calls=%async_computation.4 | async-start | bytes 18874368 | tf_op jit(solution)/shard_map/all_gather | solution.py:13
  644.6 26.6 %slice-start.1 = ((f32[896,128]{1,0:T(8,128)}), f32[128,128]{1,0:T(8,128)S(1)}, s32[]{:S(2)}) async-start(f32[896,128]{1,0:T(8,128)} %copy-done.20), calls=%async_computation.6 | async-start | bytes 131072 | tf_op jit(solution)/shard_map/slice | solution.py:74
  671.2 4.5 copy-start.26
  671.2 4.4 slice-start.2
  672.8 4.4 copy-start.2
  710.5 5.5 copy-start.15
  712.8 5.0 copy-start.4
  746.5 4.6 copy-start.28
  746.5 4.2 copy-start.8
  746.5 4.2 copy-start.14
  780.6 4.7 copy-start.31
  780.6 4.7 copy-start.13
  823.6 27.9 %copy-start.25 = (f32[256,256]{1,0:T(8,128)}, f32[256,256]{1,0:T(8,128)S(1)}, u32[]{:S(2)}) copy-start(f32[256,256]{1,0:T(8,128)S(1)} %slice_subtract_fusion.13) | copy-start | bytes 786436
  852.1 4.5 copy-start.29
  852.1 39.0 %slice-start = ((f32[128,896]{1,0:T(8,128)}), f32[128,128]{1,0:T(8,128)S(1)}, s32[]{:S(2)}) async-start(f32[128,896]{1,0:T(8,128)} %copy-done.19), calls=%async_computation.5 | async-start | bytes 131072 | tf_op jit(solution)/shard_map/slice | solution.py:78
  854.4 39.7 %slice-start.3 = ((f32[128,896]{1,0:T(8,128)}), f32[128,512]{1,0:T(8,128)S(1)}, s32[]{:S(2)}) async-start(f32[128,896]{1,0:T(8,128)} %copy-done.21), calls=%async_computation.8 | async-start | bytes 524288 | tf_op jit(solution)/shard_map/slice | solution.py:78
  891.0 4.1 copy-start.17
  891.1 4.7 copy-start.34
  895.8 13.9 %copy-start.9 = (f32[1024,1024]{1,0:T(8,128)}, f32[1024,1024]{1,0:T(8,128)S(1)}, u32[]{:S(2)}) copy-start(f32[1024,1024]{1,0:T(8,128)S(1)} %maximum_dynamic-update-slice_fusion) | copy-start | bytes 12582916
  922.5 6.7 copy-start.6
  (24 other events, 58.8 us)
Sparse Core Ops, SparseCore 0:
  59.5 87.3 all-gather.4
  176.7 148.4 all-reduce.8
  612.9 87.0 all-gather.6
